TPU v7x, 32 devices: a whole 2x2x4 slice. The times are simulated.
32 devices in a mesh: expert: 16 (over z, y, x), dp: 2 (over core).
Axes of the slice: x: 2, y: 2, z: 4, core: 2. Of those that a mesh axis runs over, the one named last changes fastest.
Arguments:
- tokens: bfloat16 [2048, 2048], P(('expert', 'dp')), may hold values from -6 to 6
- expert_ids: int32 [2048, 8], P(('expert', 'dp')), may hold values from 0 to 15, all different within a row; in each aligned block of 64 rows (0 to 63, 64 to 127, ...) at most 48 rows name the same one
- gate_probs: float32 [2048, 8], P(('expert', 'dp')), may hold values from 0.05 to 1
- swap_flags: int32 [8], replicated, may hold values from 0 to 1, as said below
- w_gate: bfloat16 [16, 2048, 768], P('expert', 'dp'), may hold values from -0.125 to 0.125
- w_up: bfloat16 [16, 2048, 768], P('expert', 'dp'), may hold values from -0.125 to 0.125
- w_down: bfloat16 [16, 768, 2048], P('expert', None, 'dp'), may hold values from -0.21875 to 0.21875
Outputs:
- moe_out: bfloat16 [2048, 2048], P(('expert', 'dp'))
Inputs may be any that keep to these rules, and one draw needn't show every extreme that they name: `expert_ids`: each row names 8 different experts. Within the 64 rows of one device no expert is named by more than 48 rows, a bound that some block reaches. swap_flags[0] is 1; the other entries are 0 or 1.
All inputs are finite; a program needn't handle non-finite values.
Results may differ from a plain program's by a relative error of at most 0.0057.
Values may be sent and summed in bfloat16 or wider, within the bound.
A program may use at most 64 MiB of HBM per device.

v0:
```python
import jax
import jax.numpy as jnp
from jax import lax
from jax.sharding import PartitionSpec as P


def on_device(tokens, expert_ids, gate_probs, swap_flags, w_gate, w_up, w_down):
    axis_size = lax.axis_size("expert")
    own_index = lax.axis_index("expert")
    half_span = axis_size // 2
    shares = gate_probs / jnp.sum(gate_probs, axis=1, keepdims=True)
    experts = jnp.arange(axis_size, dtype=jnp.int32)
    dense = jnp.sum(
        jnp.where(expert_ids[:, :, None] == experts[None, None, :], shares[:, :, None], 0.0), axis=1
    )
    lower = own_index < half_span
    own_base = jnp.where(lower, own_index, own_index - half_span)
    own_flag = (
        jnp.sum(jnp.where(jnp.arange(half_span, dtype=jnp.int32) == own_base, swap_flags, 0)) == 1
    )
    served = jnp.where(
        own_flag, jnp.where(lower, own_index + half_span, own_index - half_span), own_index
    )
    rows = lax.all_gather(tokens, "expert", axis=0, tiled=True)
    dense_all = lax.all_gather(dense, "expert", axis=0, tiled=True)
    factor = jnp.sum(jnp.where(experts[None, :] == served, dense_all, 0.0), axis=1)
    gate_next = jnp.dot(
        rows,
        lax.all_gather(w_gate, "dp", axis=1, tiled=True)[0],
        preferred_element_type=jnp.float32,
    )
    up_next = jnp.dot(
        rows, lax.all_gather(w_up, "dp", axis=1, tiled=True)[0], preferred_element_type=jnp.float32
    )
    hidden = (jax.nn.silu(gate_next) * up_next).astype(jnp.bfloat16)
    produced = jnp.dot(
        hidden,
        lax.all_gather(w_down, "dp", axis=2, tiled=True)[0],
        preferred_element_type=jnp.float32,
    ).astype(jnp.bfloat16)
    partial = (factor[:, None] * produced.astype(jnp.float32)).astype(jnp.bfloat16)
    return lax.psum_scatter(partial, "expert", scatter_dimension=0, tiled=True)


def solution(mesh):
    placed = (
        P(("expert", "dp"), None),
        P(("expert", "dp"), None),
        P(("expert", "dp"), None),
        P(),
        P("expert", "dp", None),
        P("expert", "dp", None),
        P("expert", None, "dp"),
    )
    return jax.shard_map(
        on_device, mesh=mesh, in_specs=placed, out_specs=P(("expert", "dp"), None), check_vma=False
    )
```

profile of v0, /device:TPU:0, one launch (start us, length us, event | category | flops | bytes accessed | tf_op | source)
XLA Modules:
  0.0 246.6 jit_solution(10669585378727031929)
XLA Ops:
  6.5 0.0 copy-start
  6.5 0.0 copy-start.1
  6.5 0.0 copy-start.2
  6.5 0.0 all-gather.10.cloned.1.call-start
  6.5 0.7 all-gather.10.cloned.1.call-update
  7.3 0.0 all-gather.6.cloned.1.call-start
  7.3 0.7 all-gather.6.cloned.1.call-update
  8.0 0.0 all-gather.8.cloned.1.call-start
  8.1 0.7 all-gather.8.cloned.1.call-update
  8.7 0.0 all-gather.12.cloned.1.call-start
  8.8 0.5 all-gather.12.cloned.1.call-update
  9.3 0.0 reduce-scatter.2.cloned.1.call-start
  9.4 0.0 copy-done
  9.4 0.0 copy-done.1
  9.5 43.1 %all-gather = f32[16,64,16]{1,2,0:T(8,128)S(1)} all-gather(f32[1,64,16]{1,2,0:T(8,128)S(1)} %bitcast.18), channel_id=1, replica_groups=mesh['expert'=16,'dp'=2] {'expert'}, dimensions={0}, use_global_device_ids=true | all-gather | bytes 69632 | tf_op jit(solution)/shard_map/all_gather | solution.py:25
  52.6 0.1 reshape.10
  52.7 0.0 copy-done.2
  52.7 0.6 fusion.9
  54.0 0.1 select_reduce_fusion
  54.1 0.0 all-gather.10.cloned.1.call-done
  54.1 49.5 %all-gather.6.cloned.1.call-done = bf16[1024,2048]{1,0:T(8,128)(2,1)} async-done(((bf16[64,2048]{1,0:T(8,128)(2,1)}), bf16[1024,2048]{1,0:T(8,128)(2,1)}) %all-gather.6.cloned.1.call-update) | async-done | bytes 4194320 | tf_op jit(solution)/shard_map/all_gather | solution.py:24
  103.7 6.1 %fusion.1 = f32[1024,768]{1,0:T(8,128)S(1)} fusion(bf16[1024,2048]{1,0:T(8,128)(2,1)} %all-gather.6.cloned.1.call-done, bf16[1,2048,768]{2,1,0:T(8,128)(2,1)} %all-gather.10.cloned.1.call-done), kind=kOutput, calls=%fused_computation.2 | convolution fusion | flops 3221225472 | bytes 10485760 | tf_op jit(solution)/shard_map/dot_general | solution.py:32
  109.8 6.2 %all-gather.8.cloned.1.call-done = bf16[1,2048,768]{2,1,0:T(8,128)(2,1)} async-done(((bf16[1,1024,768]{2,1,0:T(8,128)(2,1)}), bf16[1,2048,768]{2,1,0:T(8,128)(2,1)}) %all-gather.8.cloned.1.call-update) | async-done | bytes 3145744 | tf_op jit(solution)/shard_map/all_gather | solution.py:29
  116.0 14.7 %all-gather.12.cloned.1.call-done = bf16[1,768,2048]{2,1,0:T(8,128)(2,1)} async-done(((bf16[1,768,1024]{2,1,0:T(8,128)(2,1)}), bf16[1,768,2048]{2,1,0:T(8,128)(2,1)}) %all-gather.12.cloned.1.call-update) | async-done | bytes 3145744 | tf_op jit(solution)/shard_map/all_gather | solution.py:38
  130.7 12.8 %multiply_convert_fusion = bf16[1024,2048]{1,0:T(8,128)(2,1)} fusion(f32[1024]{0:T(1024)S(1)} %select_reduce_fusion, bf16[1,768,2048]{2,1,0:T(8,128)(2,1)} %all-gather.12.cloned.1.call-done, f32[1024,768]{1,0:T(8,128)S(1)} %fusion.1, bf16[1024,2048]{1,0:T(8,128)(2,1)} %all-gather.6.cloned.1.call-done, bf16[1,2048,768]{2,1,0:T(8,128)(2,1)} %all-gather.8.cloned.1.call-done), kind=kOutput, calls=%fused_computation | convolution fusion | flops 6455558144 | bytes 17829888 | tf_op jit(solution)/shard_map/dot_general | solution.py:36
  143.5 0.0 reduce-scatter.2.cloned.1.call-update
  143.6 96.5 %reduce-scatter.2.cloned.1.call-done = bf16[64,2048]{1,0:T(8,128)(2,1)} async-done(((bf16[1024,2048]{1,0:T(8,128)(2,1)}), bf16[64,2048]{1,0:T(8,128)(2,1)}) %reduce-scatter.2.cloned.1.call-update) | async-done | bytes 262160 | tf_op jit(solution)/shard_map/reduce_scatter | solution.py:42
  (5 shorter events, 0.1 us)
Async XLA Ops:
  6.5 2.8 %copy-start = (f32[64,8]{0,1:T(8,128)S(1)}, f32[64,8]{0,1:T(8,128)}, u32[]{:S(2)}) copy-start(f32[64,8]{0,1:T(8,128)} %param.9) | copy-start | bytes 6148
  6.5 2.9 %copy-start.1 = (s32[64,8]{0,1:T(8,128)S(1)}, s32[64,8]{0,1:T(8,128)}, u32[]{:S(2)}) copy-start(s32[64,8]{0,1:T(8,128)} %param.8) | copy-start | bytes 6148
  6.5 46.2 %copy-start.2 = (s32[8]{0:T(128)S(1)}, s32[8]{0:T(128)}, u32[]{:S(2)}) copy-start(s32[8]{0:T(128)} %param.10) | copy-start | bytes 100
  6.5 47.6 %all-gather.10.cloned.1.call-start = ((), (), s32[]{:S(2)}) async-start(), calls=%async_computation.3 | async-start | bytes 4718592 | tf_op jit(solution)/shard_map/all_gather | solution.py:33
  7.3 96.4 %all-gather.6.cloned.1.call-start = ((), (), s32[]{:S(2)}) async-start(), calls=%async_computation.1 | async-start | bytes 4456448 | tf_op jit(solution)/shard_map/all_gather | solution.py:24
  8.0 108.0 %all-gather.8.cloned.1.call-start = ((), (), s32[]{:S(2)}) async-start(), calls=%async_computation.2 | async-start | bytes 4718592 | tf_op jit(solution)/shard_map/all_gather | solution.py:29
  8.7 121.9 %all-gather.12.cloned.1.call-start = ((), (), s32[]{:S(2)}) async-start(), calls=%async_computation.4 | async-start | bytes 4718592 | tf_op jit(solution)/shard_map/all_gather | solution.py:38
  9.3 230.7 %reduce-scatter.2.cloned.1.call-start = ((), (), s32[]{:S(2)}) async-start(), calls=%async_computation.5 | async-start | bytes 4456448 | tf_op jit(solution)/shard_map/reduce_scatter | solution.py:42
Sparse Core Ops, SparseCore 0:
  8.9 14.8 all-gather.9
  26.5 77.0 all-gather.5
  105.2 10.7 all-gather.7
  117.4 13.2 all-gather.11
  143.7 96.3 reduce-scatter.1
where the time goes:
time: 247 us
  waiting for transfers between devices  170 us (69%)
  blocking collectives  43.1 us (17%)
  matrix products  19 us (8%)
  between operations  13.9 us (6%)
    reduce_scatter x1, waiting for transfers between devices, on_device(): return lax.psum_scatter(partial, 'expert', scatter_dimension=0, tiled=True)  96.5 us
    all_gather x1, waiting for transfers between devices, on_device(): rows = lax.all_gather(tokens, 'expert', axis=0, tiled=True)  49.5 us
    all_gather x1, blocking collectives, on_device(): dense_all = lax.all_gather(dense, 'expert', axis=0, tiled=True)  43.1 us
    all_gather x1, waiting for transfers between devices, on_device(): lax.all_gather(w_down, 'dp', axis=2, tiled=True)[0]  14.7 us
    dot_general x1, matrix products, on_device(): jnp.dot(hidden, lax.all_gather(w_down, 'dp', axis=2, tiled=True)[0], pref...  12.8 us
    all_gather x1, waiting for transfers between devices, on_device(): lax.all_gather(w_gate, 'dp', axis=1, tiled=True)[0]  6.18 us
    dot_general x1, matrix products, on_device(): jnp.dot(rows, lax.all_gather(w_up, 'dp', axis=1, tiled=True)[0], preferre...  6.12 us
  transfers between devices with their start and end apart: 5, of which 4 were waited for; matrix products, arithmetic and copies ran while one was open for 3% of the time, Pallas kernels for 0%

commit v1 on v0

--- a/solution.py
+++ b/solution.py
@@ -21,8 +21,11 @@
     served = jnp.where(
         own_flag, jnp.where(lower, own_index + half_span, own_index - half_span), own_index
     )
-    rows = lax.all_gather(tokens, "expert", axis=0, tiled=True)
-    dense_all = lax.all_gather(dense, "expert", axis=0, tiled=True)
+    rows, dense_all = jnp.split(
+        lax.all_gather(jnp.concatenate([tokens, dense], axis=1), "expert", axis=0, tiled=True),
+        [tokens.shape[1]],
+        axis=1,
+    )
     factor = jnp.sum(jnp.where(experts[None, :] == served, dense_all, 0.0), axis=1)
     gate_next = jnp.dot(
         rows,

time: 247 us -> 289 us (1.17)
  waiting for transfers between devices: 170 us -> 249 us
  blocking collectives: 43.1 us -> 0 us
  other arithmetic: 0.77 us -> 5.81 us
    all_gather x1, waiting for transfers between devices: 49.5 us -> 117 us  [on_device(): lax.all_gather(jnp.concatenate([tokens, dense], axis=1), 'expert', axis=0...]
    all_gather x1 -> x0, blocking collectives: 43.1 us -> none  [on_device(): dense_all = lax.all_gather(dense, 'expert', axis=0, tiled=True)]
    all_gather x1, waiting for transfers between devices: 0.02 us -> 8.1 us  [on_device(): lax.all_gather(w_up, 'dp', axis=1, tiled=True)[0]]
    all_gather x1, waiting for transfers between devices: 6.18 us -> 10.6 us  [on_device(): lax.all_gather(w_gate, 'dp', axis=1, tiled=True)[0]]
  transfers between devices with their start and end apart: 5 -> 5, of which waited for: 4 -> 5; matrix products, arithmetic and copies ran while one was open for 3% -> 3% of each run, Pallas kernels for 0% -> 0%
where the time goes in v1:
time: 289 us
  waiting for transfers between devices  249 us (86%)
  matrix products  20.2 us (7%)
  between operations  13.8 us (5%)
  other arithmetic  5.81 us (2%)
    all_gather x1, waiting for transfers between devices, on_device(): lax.all_gather(jnp.concatenate([tokens, dense], axis=1), 'expert', axis=0...  117 us
    reduce_scatter x1, waiting for transfers between devices, on_device(): return lax.psum_scatter(partial, 'expert', scatter_dimension=0, tiled=True)  96.4 us
    all_gather x1, waiting for transfers between devices, on_device(): lax.all_gather(w_down, 'dp', axis=2, tiled=True)[0]  14.7 us
    dot_general x1, matrix products, on_device(): jnp.dot(hidden, lax.all_gather(w_down, 'dp', axis=2, tiled=True)[0], pref...  13.4 us
    all_gather x1, waiting for transfers between devices, on_device(): lax.all_gather(w_gate, 'dp', axis=1, tiled=True)[0]  10.6 us
    all_gather x1, waiting for transfers between devices, on_device(): lax.all_gather(w_up, 'dp', axis=1, tiled=True)[0]  8.1 us
    dot_general x1, matrix products, on_device(): jnp.dot(rows, lax.all_gather(w_gate, 'dp', axis=1, tiled=True)[0], prefer...  6.77 us
  transfers between devices with their start and end apart: 5, of which 5 were waited for; matrix products, arithmetic and copies ran while one was open for 3% of the time, Pallas kernels for 0%

profile of v1, /device:TPU:0, one launch (start us, length us, event | category | flops | bytes accessed | tf_op | source)
XLA Modules:
  0.0 289.1 jit_solution(15684480819451755601)
XLA Ops:
  6.5 0.0 all-gather.5.cloned.1.call-start
  6.5 0.7 reduce_sum.37
  7.2 0.7 broadcast_divide_fusion
  7.9 0.7 select_reduce_fusion
  8.6 0.1 copy.10
  8.7 1.0 convert_element_type.15
  9.7 0.0 copy-start
  9.7 0.8 pad_maximum_fusion
  10.6 0.0 all-gather.5.cloned.1.call-update
  10.6 0.0 all-gather.7.cloned.1.call-start
  10.6 0.7 all-gather.7.cloned.1.call-update
  11.3 0.0 all-gather.9.cloned.1.call-start
  11.4 0.7 all-gather.9.cloned.1.call-update
  12.1 0.0 all-gather.11.cloned.1.call-start
  12.1 0.5 all-gather.11.cloned.1.call-update
  12.7 0.0 reduce-scatter.2.cloned.1.call-start
  12.7 0.0 copy-done
  12.7 0.6 fusion.16
  14.0 117.1 %all-gather.5.cloned.1.call-done = f32[1024,2064]{1,0:T(8,128)} async-done(((f32[64,2064]{1,0:T(8,128)}), f32[1024,2064]{1,0:T(8,128)}) %all-gather.5.cloned.1.call-update) | async-done | bytes 8454160 | tf_op jit(solution)/shard_map/all_gather | solution.py:25
  131.2 1.2 fusion.15
  132.4 10.6 %all-gather.7.cloned.1.call-done = bf16[1,2048,768]{2,1,0:T(8,128)(2,1)} async-done(((bf16[1,1024,768]{2,1,0:T(8,128)(2,1)}), bf16[1,2048,768]{2,1,0:T(8,128)(2,1)}) %all-gather.7.cloned.1.call-update) | async-done | bytes 3145744 | tf_op jit(solution)/shard_map/all_gather | solution.py:32
  143.1 6.8 %fusion.2 = f32[1024,768]{1,0:T(8,128)S(1)} fusion(f32[1024,2064]{1,0:T(8,128)} %all-gather.5.cloned.1.call-done, bf16[1,2048,768]{2,1,0:T(8,128)(2,1)} %all-gather.7.cloned.1.call-done), kind=kOutput, calls=%fused_computation.3 | convolution fusion | flops 3221225472 | bytes 10485760 | tf_op jit(solution)/shard_map/dot_general | solution.py:30
  149.8 8.1 %all-gather.9.cloned.1.call-done = bf16[1,2048,768]{2,1,0:T(8,128)(2,1)} async-done(((bf16[1,1024,768]{2,1,0:T(8,128)(2,1)}), bf16[1,2048,768]{2,1,0:T(8,128)(2,1)}) %all-gather.9.cloned.1.call-update) | async-done | bytes 3145744 | tf_op jit(solution)/shard_map/all_gather | solution.py:36
  157.9 14.7 %all-gather.11.cloned.1.call-done = bf16[1,768,2048]{2,1,0:T(8,128)(2,1)} async-done(((bf16[1,768,1024]{2,1,0:T(8,128)(2,1)}), bf16[1,768,2048]{2,1,0:T(8,128)(2,1)}) %all-gather.11.cloned.1.call-update) | async-done | bytes 3145744 | tf_op jit(solution)/shard_map/all_gather | solution.py:41
  172.7 13.4 %multiply_convert_fusion = bf16[1024,2048]{1,0:T(8,128)(2,1)} fusion(f32[1024]{0:T(1024)S(1)} %fusion.15, bf16[1,768,2048]{2,1,0:T(8,128)(2,1)} %all-gather.11.cloned.1.call-done, f32[1024,768]{1,0:T(8,128)S(1)} %fusion.2, bf16[1,2048,768]{2,1,0:T(8,128)(2,1)} %all-gather.9.cloned.1.call-done, f32[1024,2064]{1,0:T(8,128)} %all-gather.5.cloned.1.call-done), kind=kOutput, calls=%fused_computation | convolution fusion | flops 6455558144 | bytes 17829888 | tf_op jit(solution)/shard_map/dot_general | solution.py:39
  186.1 0.0 reduce-scatter.2.cloned.1.call-update
  186.1 96.4 %reduce-scatter.2.cloned.1.call-done = bf16[64,2048]{1,0:T(8,128)(2,1)} async-done(((bf16[1024,2048]{1,0:T(8,128)(2,1)}), bf16[64,2048]{1,0:T(8,128)(2,1)}) %reduce-scatter.2.cloned.1.call-update) | async-done | bytes 262160 | tf_op jit(solution)/shard_map/reduce_scatter | solution.py:45
  (1 shorter events, 0.0 us)
Async XLA Ops:
  6.5 124.6 %all-gather.5.cloned.1.call-start = ((), (), s32[]{:S(2)}) async-start(), calls=%async_computation.1 | async-start | bytes 9469952 | tf_op jit(solution)/shard_map/all_gather | solution.py:25
  9.7 3.0 %copy-start = (s32[8]{0:T(128)S(1)}, s32[8]{0:T(128)}, u32[]{:S(2)}) copy-start(s32[8]{0:T(128)} %param.10) | copy-start | bytes 100
  10.6 132.5 %all-gather.7.cloned.1.call-start = ((), (), s32[]{:S(2)}) async-start(), calls=%async_computation.2 | async-start | bytes 4718592 | tf_op jit(solution)/shard_map/all_gather | solution.py:32
  11.3 146.6 %all-gather.9.cloned.1.call-start = ((), (), s32[]{:S(2)}) async-start(), calls=%async_computation.3 | async-start | bytes 4718592 | tf_op jit(solution)/shard_map/all_gather | solution.py:36
  12.1 160.6 %all-gather.11.cloned.1.call-start = ((), (), s32[]{:S(2)}) async-start(), calls=%async_computation.4 | async-start | bytes 4718592 | tf_op jit(solution)/shard_map/all_gather | solution.py:41
  12.7 269.9 %reduce-scatter.2.cloned.1.call-start = ((), (), s32[]{:S(2)}) async-start(), calls=%async_computation.5 | async-start | bytes 4456448 | tf_op jit(solution)/shard_map/reduce_scatter | solution.py:45
Sparse Core Ops, SparseCore 0:
  10.7 120.4 all-gather.4
  132.7 10.3 all-gather.6
  144.6 13.2 all-gather.8
  159.3 13.2 all-gather.10
  186.2 96.2 reduce-scatter.1
